TPU v7x, 32 devices: a whole 2x2x4 slice. The times are simulated.
32 devices in a mesh: rep: 4 (over x, core), fsdp: 2 (over y), seq: 4 (over z).
Axes of the slice: x: 2, y: 2, z: 4, core: 2. Of those that a mesh axis runs over, the one named last changes fastest.
Arguments:
- tokens: bfloat16 [8, 512, 1024], P(('rep', 'fsdp'), 'seq'), may hold values from -6 to 6
- conditioning: bfloat16 [8, 1024], P(('rep', 'fsdp')), may hold values from -6 to 6
- cotangent: bfloat16 [8, 512, 1024], P(('rep', 'fsdp'), 'seq'), may hold values from -6 to 6
- ada_weight: bfloat16 [1024, 6144], P('fsdp'), may hold values from -0.1875 to 0.1875
- ada_bias: bfloat16 [6144], P('fsdp'), may hold values from -3 to 3
- qkv_weight: bfloat16 [1024, 3072], P('fsdp'), may hold values from -0.1875 to 0.1875
- qv_bias: bfloat16 [2048], P('fsdp'), may hold values from -3 to 3
- proj_weight: bfloat16 [1024, 1024], P('fsdp'), may hold values from -1 to 1
- proj_bias: bfloat16 [1024], P('fsdp'), may hold values from -3 to 3
- fc1_weight: bfloat16 [1024, 4096], P('fsdp'), may hold values from -0.1875 to 0.1875
- fc1_bias: bfloat16 [4096], P('fsdp'), may hold values from -3 to 3
- fc2_weight: bfloat16 [4096, 1024], P('fsdp'), may hold values from -0.09375 to 0.09375
- fc2_bias: bfloat16 [1024], P('fsdp'), may hold values from -3 to 3
Outputs:
- output: bfloat16 [8, 512, 1024], P(('rep', 'fsdp'), 'seq')
- tokens_grad: float32 [8, 512, 1024], P(('rep', 'fsdp'), 'seq')
- cond_grad: float32 [8, 1024], P(('rep', 'fsdp'))
- ada_weight_grad: float32 [1024, 6144], P('fsdp')
- ada_bias_grad: float32 [6144], P('fsdp')
- qkv_weight_grad: float32 [1024, 3072], P('fsdp')
- qv_bias_grad: float32 [2048], P('fsdp')
- proj_weight_grad: float32 [1024, 1024], P('fsdp')
- proj_bias_grad: float32 [1024], P('fsdp')
- fc1_weight_grad: float32 [1024, 4096], P('fsdp')
- fc1_bias_grad: float32 [4096], P('fsdp')
- fc2_weight_grad: float32 [4096, 1024], P('fsdp')
- fc2_bias_grad: float32 [1024], P('fsdp')
All inputs are finite; a program needn't handle non-finite values.
Results may differ from a plain program's by a relative error of at most 0.012.
The roundings to bfloat16 on the way count: a program that leaves them out, or rounds other values in their place, can miss the bound.
Values may be sent and summed in bfloat16 or wider, within the bound.
No kernel may reach another device: no remote copies, remote signals or barrier semaphores. Data moves between devices by JAX's collectives and lax.ppermute only.
A program may use at most 256 MiB of HBM per device.

v0:
```python
import jax
import jax.numpy as jnp
from jax import lax
from jax.sharding import PartitionSpec as P

HEADS = 16
HEAD_DIM = 64
EPSILON = 1e-06
TANH_ROOT = 0.7978845608028654
CUBIC_COEF = 0.044715


def product(left_op, right_op):
    return jnp.dot(left_op, right_op, preferred_element_type=jnp.float32)


def product_tn(left_op, right_op):
    return lax.dot_general(
        left_op, right_op, (((0,), (0,)), ((), ())), preferred_element_type=jnp.float32
    )


def product_nt(left_op, right_op):
    return lax.dot_general(
        left_op, right_op, (((1,), (1,)), ((), ())), preferred_element_type=jnp.float32
    )


def gelu_parts(pre_act):
    tanh_val = jnp.tanh(TANH_ROOT * (pre_act + CUBIC_COEF * pre_act * pre_act * pre_act))
    gelu_val = 0.5 * pre_act * (1.0 + tanh_val)
    gelu_slope = 0.5 * (1.0 + tanh_val) + 0.5 * pre_act * (
        1.0 - tanh_val * tanh_val
    ) * TANH_ROOT * (1.0 + 3.0 * CUBIC_COEF * pre_act * pre_act)
    return (gelu_val, gelu_slope)


def layer_norm(values):
    center = values - jnp.mean(values, axis=-1, keepdims=True)
    inv_std = lax.rsqrt(jnp.mean(center * center, axis=-1, keepdims=True) + EPSILON)
    return (center * inv_std, inv_std)


def norm_back(normed, inv_std, grad_in):
    return inv_std * (
        grad_in
        - jnp.mean(grad_in, axis=-1, keepdims=True)
        - normed * jnp.mean(grad_in * normed, axis=-1, keepdims=True)
    )


def silu_slope(condition):
    sigmoid_c = jax.nn.sigmoid(condition)
    return sigmoid_c * (1.0 + condition * (1.0 - sigmoid_c))


def split_heads(values):
    return values.reshape(values.shape[0], HEADS, values.shape[1] // HEADS)


def attend(query_rows, key_rows, value_rows):
    score_scale = HEAD_DIM ** (-0.5)
    scores = (
        jnp.einsum(
            "qhd,khd->hqk",
            split_heads(query_rows),
            split_heads(key_rows),
            preferred_element_type=jnp.float32,
        )
        * score_scale
    )
    row_max = jnp.max(scores, axis=-1, keepdims=True)
    exponent = jnp.exp(scores - row_max)
    row_total = jnp.sum(exponent, axis=-1, keepdims=True)
    attn_probs = (exponent / row_total).astype(jnp.bfloat16)
    attended = jnp.einsum(
        "hqk,khd->qhd", attn_probs, split_heads(value_rows), preferred_element_type=jnp.float32
    )
    attended = attended.reshape(query_rows.shape[0], query_rows.shape[1]).astype(jnp.bfloat16)
    return (attended, row_max + jnp.log(row_total))


def attend_back(query_rows, key_rows, value_rows, log_total, attended_grad):
    score_scale = HEAD_DIM ** (-0.5)
    query_heads, key_heads, value_heads = (
        split_heads(query_rows),
        split_heads(key_rows),
        split_heads(value_rows),
    )
    grad_heads = split_heads(attended_grad)
    scores = (
        jnp.einsum("qhd,khd->hqk", query_heads, key_heads, preferred_element_type=jnp.float32)
        * score_scale
    )
    probs_again = jnp.exp(scores - log_total)
    value_grad = jnp.einsum(
        "hqk,qhd->khd",
        probs_again.astype(jnp.bfloat16),
        grad_heads,
        preferred_element_type=jnp.float32,
    )
    prob_grad = jnp.einsum(
        "qhd,khd->hqk", grad_heads, value_heads, preferred_element_type=jnp.float32
    )
    row_delta = jnp.sum(probs_again * prob_grad, axis=-1, keepdims=True)
    score_grad = (probs_again * (prob_grad - row_delta) * score_scale).astype(jnp.bfloat16)
    query_grad = jnp.einsum(
        "hqk,khd->qhd", score_grad, key_heads, preferred_element_type=jnp.float32
    )
    key_grad = jnp.einsum(
        "hqk,qhd->khd", score_grad, query_heads, preferred_element_type=jnp.float32
    )
    model_width = query_rows.shape[1]
    return (
        query_grad.reshape(query_rows.shape[0], model_width),
        key_grad.reshape(key_rows.shape[0], model_width),
        value_grad.reshape(key_rows.shape[0], model_width),
    )


def local(
    tokens,
    conditioning,
    cotangent,
    ada_weight,
    ada_bias,
    qkv_weight,
    qv_bias,
    proj_weight,
    proj_bias,
    fc1_weight,
    fc1_bias,
    fc2_weight,
    fc2_bias,
):
    local_tokens = tokens[0]
    model_width = local_tokens.shape[1]
    cond_f = conditioning.astype(jnp.float32)
    silu_cond = jax.nn.silu(cond_f).astype(jnp.bfloat16)
    (
        qkv_full,
        qv_full,
        proj_full,
        projb_full,
        fc1_full,
        fc1b_full,
        fc2_full,
        fc2b_full,
        adab_full,
    ) = (
        lax.all_gather(qkv_weight, "fsdp", axis=0, tiled=True),
        lax.all_gather(qv_bias, "fsdp", axis=0, tiled=True),
        lax.all_gather(proj_weight, "fsdp", axis=0, tiled=True),
        lax.all_gather(proj_bias, "fsdp", axis=0, tiled=True),
        lax.all_gather(fc1_weight, "fsdp", axis=0, tiled=True),
        lax.all_gather(fc1_bias, "fsdp", axis=0, tiled=True),
        lax.all_gather(fc2_weight, "fsdp", axis=0, tiled=True),
        lax.all_gather(fc2_bias, "fsdp", axis=0, tiled=True),
        lax.all_gather(ada_bias, "fsdp", axis=0, tiled=True),
    )
    share = ada_weight.shape[0]
    groups = lax.axis_size("fsdp")
    cond_all = lax.all_gather(silu_cond, "fsdp", axis=0, tiled=True)
    own_cols = lax.dynamic_slice_in_dim(cond_all, lax.axis_index("fsdp") * share, share, 1)
    mods = lax.psum_scatter(product(own_cols, ada_weight), "fsdp", scatter_dimension=0, tiled=True)[
        0
    ]
    mods = mods + adab_full.astype(jnp.float32)
    shift_attn, scale_attn, gate_attn, shift_mlp, scale_mlp, gate_mlp = jnp.split(mods, 6)
    tokens_f = local_tokens.astype(jnp.float32)
    normed1, inv_std1 = layer_norm(tokens_f)
    hidden1 = (normed1 * (1.0 + scale_attn) + shift_attn).astype(jnp.bfloat16)
    qkv_rows = product(hidden1, qkv_full)
    qv_float = qv_full.astype(jnp.float32)
    query_rows = (qkv_rows[:, :model_width] + qv_float[:model_width]).astype(jnp.bfloat16)
    key_rows = qkv_rows[:, model_width : 2 * model_width].astype(jnp.bfloat16)
    value_rows = (qkv_rows[:, 2 * model_width :] + qv_float[model_width:]).astype(jnp.bfloat16)
    key_all, value_all = (
        lax.all_gather(key_rows, "seq", axis=0, tiled=True),
        lax.all_gather(value_rows, "seq", axis=0, tiled=True),
    )
    attended, log_total = attend(query_rows, key_all, value_all)
    branch = product(attended, proj_full) + projb_full.astype(jnp.float32)
    middle = tokens_f + gate_attn * branch
    normed2, inv_std2 = layer_norm(middle)
    hidden2 = (normed2 * (1.0 + scale_mlp) + shift_mlp).astype(jnp.bfloat16)
    pre_act = product(hidden2, fc1_full) + fc1b_full.astype(jnp.float32)
    gelu_val, gelu_slope = gelu_parts(pre_act)
    active = gelu_val.astype(jnp.bfloat16)
    mlp_out = product(active, fc2_full) + fc2b_full.astype(jnp.float32)
    output = (middle + gate_mlp * mlp_out).astype(jnp.bfloat16)
    qkv_back, proj_back, fc1_back, fc2_back = (
        lax.all_gather(qkv_weight, "fsdp", axis=0, tiled=True),
        lax.all_gather(proj_weight, "fsdp", axis=0, tiled=True),
        lax.all_gather(fc1_weight, "fsdp", axis=0, tiled=True),
        lax.all_gather(fc2_weight, "fsdp", axis=0, tiled=True),
    )
    cot_f = cotangent[0].astype(jnp.float32)
    mlp_grad = (gate_mlp * cot_f).astype(jnp.bfloat16)
    gate_mlp_grad = jnp.sum(cot_f * mlp_out, axis=0)
    pre_grad = (product_nt(mlp_grad, fc2_back) * gelu_slope).astype(jnp.bfloat16)
    fc1_bias_grad = jnp.sum(pre_grad.astype(jnp.float32), axis=0)
    hidden2_grad = product_nt(pre_grad, fc1_back)
    shift_mlp_grad = jnp.sum(hidden2_grad, axis=0)
    scale_mlp_grad = jnp.sum(hidden2_grad * normed2, axis=0)
    middle_grad = cot_f + norm_back(normed2, inv_std2, hidden2_grad * (1.0 + scale_mlp))
    gate_attn_grad = jnp.sum(middle_grad * branch, axis=0)
    branch_grad = (gate_attn * middle_grad).astype(jnp.bfloat16)
    attended_grad = product_nt(branch_grad, proj_back).astype(jnp.bfloat16)
    query_grad, key_part, value_part = attend_back(
        query_rows, key_all, value_all, log_total, attended_grad
    )
    key_grad, value_grad = (
        lax.psum_scatter(key_part, "seq", scatter_dimension=0, tiled=True),
        lax.psum_scatter(value_part, "seq", scatter_dimension=0, tiled=True),
    )
    query_b = query_grad.astype(jnp.bfloat16)
    value_b = value_grad.astype(jnp.bfloat16)
    qkv_grad = jnp.concatenate([query_b, key_grad.astype(jnp.bfloat16), value_b], axis=1)
    qv_bias_grad = jnp.concatenate(
        [jnp.sum(query_b.astype(jnp.float32), axis=0), jnp.sum(value_b.astype(jnp.float32), axis=0)]
    )
    hidden1_grad = product_nt(qkv_grad, qkv_back)
    shift_attn_grad = jnp.sum(hidden1_grad, axis=0)
    scale_attn_grad = jnp.sum(hidden1_grad * normed1, axis=0)
    tokens_grad = middle_grad + norm_back(normed1, inv_std1, hidden1_grad * (1.0 + scale_attn))
    mods_grad = jnp.concatenate(
        [
            shift_attn_grad,
            scale_attn_grad,
            gate_attn_grad,
            shift_mlp_grad,
            scale_mlp_grad,
            gate_mlp_grad,
        ]
    )
    proj_bias_grad = jnp.sum(branch_grad.astype(jnp.float32), axis=0)
    fc2_bias_grad = jnp.sum(mlp_grad.astype(jnp.float32), axis=0)
    hidden1_cols, hidden2_cols, active_cols, attended_cols = (
        lax.all_to_all(hidden1, "fsdp", split_axis=1, concat_axis=0, tiled=True),
        lax.all_to_all(hidden2, "fsdp", split_axis=1, concat_axis=0, tiled=True),
        lax.all_to_all(active, "fsdp", split_axis=1, concat_axis=0, tiled=True),
        lax.all_to_all(attended, "fsdp", split_axis=1, concat_axis=0, tiled=True),
    )
    qkv_all, pre_all, mlp_all, branch_all = (
        lax.all_gather(qkv_grad, "fsdp", axis=0, tiled=True),
        lax.all_gather(pre_grad, "fsdp", axis=0, tiled=True),
        lax.all_gather(mlp_grad, "fsdp", axis=0, tiled=True),
        lax.all_gather(branch_grad, "fsdp", axis=0, tiled=True),
    )
    qkv_shard = product_tn(hidden1_cols, qkv_all)
    fc1_shard = product_tn(hidden2_cols, pre_all)
    fc2_shard = product_tn(active_cols, mlp_all)
    proj_shard = product_tn(attended_cols, branch_all)
    qv_shard, projb_shard, fc1b_shard, fc2b_shard, adab_shard = (
        lax.psum_scatter(qv_bias_grad, "fsdp", scatter_dimension=0, tiled=True),
        lax.psum_scatter(proj_bias_grad, "fsdp", scatter_dimension=0, tiled=True),
        lax.psum_scatter(fc1_bias_grad, "fsdp", scatter_dimension=0, tiled=True),
        lax.psum_scatter(fc2_bias_grad, "fsdp", scatter_dimension=0, tiled=True),
        lax.psum_scatter(mods_grad, "fsdp", scatter_dimension=0, tiled=True),
    )
    mod_rows = lax.all_gather(mods_grad[None, :], ("fsdp", "seq"), axis=0, tiled=True)
    stacked = mod_rows.reshape(groups, mod_rows.shape[0] // groups, mod_rows.shape[1])
    own_seq = lax.dynamic_index_in_dim(stacked, lax.axis_index("seq"), 1, keepdims=False)
    ada_shard = lax.dot_general(
        own_cols.astype(jnp.float32),
        own_seq,
        (((0,), (0,)), ((), ())),
        precision=lax.Precision.HIGHEST,
    )
    cond_part = lax.dot_general(
        jnp.sum(stacked, axis=1),
        ada_weight.astype(jnp.float32),
        (((1,), (1,)), ((), ())),
        precision=lax.Precision.HIGHEST,
    )
    cond_sum = lax.all_to_all(cond_part, "fsdp", split_axis=0, concat_axis=1, tiled=True)
    cond_grad = cond_sum * silu_slope(cond_f)
    sums = lax.psum(
        (
            ada_shard,
            adab_shard,
            qkv_shard,
            qv_shard,
            proj_shard,
            projb_shard,
            fc1_shard,
            fc1b_shard,
            fc2_shard,
            fc2b_shard,
        ),
        ("rep", "seq"),
    )
    return (
        output[None],
        tokens_grad[None],
        cond_grad,
        sums[0],
        sums[1],
        sums[2],
        sums[3],
        sums[4],
        sums[5],
        sums[6],
        sums[7],
        sums[8],
        sums[9],
    )


def solution(mesh):
    in_specs = (
        P(("rep", "fsdp"), "seq", None),
        P(("rep", "fsdp"), None),
        P(("rep", "fsdp"), "seq", None),
        P("fsdp", None),
        P("fsdp"),
        P("fsdp", None),
        P("fsdp"),
        P("fsdp", None),
        P("fsdp"),
        P("fsdp", None),
        P("fsdp"),
        P("fsdp", None),
        P("fsdp"),
    )
    out_specs = (
        P(("rep", "fsdp"), "seq", None),
        P(("rep", "fsdp"), "seq", None),
        P(("rep", "fsdp"), None),
        P("fsdp", None),
        P("fsdp"),
        P("fsdp", None),
        P("fsdp"),
        P("fsdp", None),
        P("fsdp"),
        P("fsdp", None),
        P("fsdp"),
        P("fsdp", None),
        P("fsdp"),
    )
    return jax.shard_map(local, mesh=mesh, in_specs=in_specs, out_specs=out_specs, check_vma=False)
```

profile of v0, /device:TPU:0, one launch (start us, length us, event | category | flops | bytes accessed | tf_op | source)
XLA Modules:
  0.0 1255.6 jit_solution(5859581527247387863)
XLA Ops:
  8.0 1.2 dynamic-slice.1
  9.2 5.5 all_gather.58
  15.4 4.4 all-gather.1
  19.8 4.6 all_gather.56
  24.4 4.3 fusion.54
  28.7 10.4 all-reduce
  40.2 53.5 %all-gather.13.cloned.1.call-done = bf16[1024,3072]{1,0:T(8,128)(2,1)} async-done(((bf16[512,3072]{1,0:T(8,128)(2,1)}), bf16[1024,3072]{1,0:T(8,128)(2,1)}) %all-gather.13.cloned.1.call-update) | async-done | bytes 6291472 | tf_op jit(solution)/shard_map/all_gather | solution.py:151
  93.7 3.9 fusion.44
  101.1 4.4 all-gather.2
  105.5 4.4 all-gather.3
  109.9 4.8 all_gather.64
  115.0 11.7 all-gather.15.cloned.1.call-done
  126.6 1.5 copy.51
  128.1 28.0 %all-gather.17.cloned.1.call-done = bf16[512,1024]{1,0:T(8,128)(2,1)} async-done(((bf16[128,1024]{1,0:T(8,128)(2,1)}), bf16[512,1024]{1,0:T(8,128)(2,1)}) %all-gather.17.cloned.1.call-update) | async-done | bytes 1048592 | tf_op jit(solution)/shard_map/all_gather | solution.py:179
  156.2 1.5 copy.53
  158.5 1.2 fusion.3
  160.5 2.2 fusion.31
  162.7 27.3 %all-gather.19.cloned.1.call-done = bf16[1024,1024]{1,0:T(8,128)(2,1)} async-done(((bf16[512,1024]{1,0:T(8,128)(2,1)}), bf16[1024,1024]{1,0:T(8,128)(2,1)}) %all-gather.19.cloned.1.call-update) | async-done | bytes 2097168 | tf_op jit(solution)/shard_map/all_gather | solution.py:153
  190.1 3.0 fusion.68
  193.3 0.9 add_convert_fusion.1
  194.1 101.3 %all-gather.21.cloned.1.call-done = bf16[1024,4096]{1,0:T(8,128)(2,1)} async-done(((bf16[512,4096]{1,0:T(8,128)(2,1)}), bf16[1024,4096]{1,0:T(8,128)(2,1)}) %all-gather.21.cloned.1.call-update) | async-done | bytes 8388624 | tf_op jit(solution)/shard_map/all_gather | solution.py:155
  295.5 6.7 multiply_convert_fusion.1
  302.1 98.7 %all-gather.23.cloned.1.call-done = bf16[4096,1024]{1,0:T(8,128)(2,1)} async-done(((bf16[2048,1024]{1,0:T(8,128)(2,1)}), bf16[4096,1024]{1,0:T(8,128)(2,1)}) %all-gather.23.cloned.1.call-update) | async-done | bytes 8388624 | tf_op jit(solution)/shard_map/all_gather | solution.py:157
  400.9 8.5 convert_reduce_fusion
  409.6 6.9 multiply_reduce_fusion.2
  416.5 2.4 fusion.36
  420.0 4.5 fusion.13
  424.6 4.0 fusion.73
  428.6 18.3 %fusion.8 = f32[16,64,512]{2,1,0:T(8,128)} fusion(bf16[128,16,64]{0,2,1:T(8,128)(2,1)S(1)} %bitcast.135, f32[16,128,512]{2,1,0:T(8,128)} %fusion.73, f32[16,128,512]{2,1,0:T(8,128)} %copy-done, f32[16,128]{1,0:T(8,128)S(1)} %log_add_fusion), kind=kOutput, calls=%fused_computation.15 | convolution fusion | flops 143657472 | bytes 10756096 | tf_op jit(solution)/shard_map/hqk,qhd->khd/dot_general | solution.py:110
  446.9 1.3 reshape.183
  448.2 8.5 all_gather.71
  456.7 2.1 fusion.42
  458.8 1.8 copy.57
  460.6 3.4 all-to-all-start.2
  464.1 1.7 copy.88
  465.8 1.0 copy.87
  466.8 8.2 all_gather.69
  475.7 3.6 all-to-all-start.4
  479.3 18.0 %convert_reduce_fusion.4 = (f32[16,64]{1,0:T(8,128)S(1)}, bf16[16,64,128]{2,1,0:T(8,128)(2,1)}) fusion(bf16[512,16,64]{0,2,1:T(8,128)(2,1)S(1)} %bitcast.122, f32[16,128,512]{2,1,0:T(8,128)} %fusion.73, f32[16,128,512]{2,1,0:T(8,128)} %copy-done, f32[16,128]{1,0:T(8,128)S(1)} %log_add_fusion), kind=kOutput, calls=%fused_computation.60 | convolution fusion | flops 144049664 | bytes 9711616 | tf_op jit(solution)/shard_map/hqk,khd->qhd/dot_general | solution.py:107
  497.3 2.8 fusion.75
  500.0 3.7 all-to-all-start.3
  503.7 4.7 fusion.77
  508.9 3.4 all-to-all-start.1
  512.4 6.3 fusion.76
  518.7 1.2 convert_reduce_fusion.3
  520.0 14.9 %reduce-scatter.3.cloned.1.call-done = f32[128,1024]{0,1:T(8,128)} async-done(((f32[512,1024]{0,1:T(8,128)}), f32[128,1024]{0,1:T(8,128)}) %reduce-scatter.3.cloned.1.call-update) | async-done | bytes 524304 | tf_op jit(solution)/shard_map/reduce_scatter | solution.py:214
  534.9 1.1 convert_element_type.161
  536.0 0.9 pad_maximum_fusion
  537.0 5.2 multiply_reduce_fusion.4
  542.3 1.1 multiply_reduce_fusion.3
  543.4 31.1 %all-gather = f32[49152]{0:T(1024)S(1)} all-gather(f32[6144]{0:T(1024)S(1)} %constant_dynamic-update-slice_fusion), channel_id=2, replica_groups=mesh['rep'=4,'fsdp'=2,'seq'=4] {'fsdp','seq'}, dimensions={0}, use_global_device_ids=true | all-gather | bytes 221184 | tf_op jit(solution)/shard_map/all_gather | solution.py:262
  574.6 8.0 fusion.50
  582.7 5.1 fusion.74
  590.6 8.8 all-reduce.8
  599.7 7.1 convolution_bitcast_fusion
  607.3 3.2 all-to-all-start
  610.6 62.2 %all-reduce.6 = (f32[3072]{0:T(1024)}, f32[1024]{0:T(1024)}, f32[512]{0:T(512)}, f32[2048]{0:T(1024)}, f32[512]{0:T(512)}) all-reduce(f32[3072]{0:T(1024)S(1)} %dynamic-slice.4, f32[1024]{0:T(1024)S(1)} %dynamic-slice.6, f32[512]{0:T(512)S(1)} %dynamic-slice.8, ...), channel_id=1, replica_groups=mesh['rep'=4,'fsdp'=2,'seq'=4] {'rep','seq'}, use_global_device_ids=true, to_apply=%region_23.24 | all-reduce | flops 7168 | bytes 57344 | tf_op jit(solution)/shard_map/psum | solution.py:279
  673.4 546.8 %all-reduce.11.cloned.1.call-done = (f32[512,6144]{1,0:T(8,128)}, f32[512,3072]{1,0:T(8,128)}, f32[512,1024]{1,0:T(8,128)}, f32[512,4096]{1,0:T(8,128)}, f32[2048,1024]{1,0:T(8,128)}) async-done(((f32[512,6144]{1,0:T(8,128)}, f32[512,3072]{1,0:T(8,128)}, f32[512,1024]{1,0:T(8,128)}, f32[512,4096]{1,0:T(8,128)}, f32[2048,1024]{1,0:T(8,128)}), (f32[512,6144]{1,0:T(8,128)}, f32[512,3072]{1,0:T(8,128)}, ...) | async-done | bytes 37748752 | tf_op jit(solution)/shard_map/psum | solution.py:279
  1220.2 10.8 copy.99
  1231.0 6.9 copy.100
  1237.9 1.3 copy.101
  1239.7 4.3 copy.102
  1243.9 1.5 slice-done.1
  1245.4 3.4 copy.103
  (125 shorter events, 12.9 us)
Async XLA Ops:
  7.2 31.9 %copy-start.2 = (bf16[1,128,1024]{2,1,0:T(8,128)(2,1)S(1)}, bf16[1,128,1024]{2,1,0:T(8,128)(2,1)}, u32[]{:S(2)}) copy-start(bf16[1,128,1024]{2,1,0:T(8,128)(2,1)} %param.13) | copy-start | bytes 786436
  7.2 86.5 %all-gather.13.cloned.1.call-start = ((), (), s32[]{:S(2)}) async-start(), calls=%async_computation.7 | async-start | bytes 9437184 | tf_op jit(solution)/shard_map/all_gather | solution.py:151
  7.9 118.7 %all-gather.15.cloned.1.call-start = ((), (), s32[]{:S(2)}) async-start(), calls=%async_computation.8 | async-start | bytes 1310720 | tf_op jit(solution)/shard_map/all_gather | solution.py:180
  98.4 57.7 %all-gather.17.cloned.1.call-start = ((), (), s32[]{:S(2)}) async-start(), calls=%async_computation.9 | async-start | bytes 1310720 | tf_op jit(solution)/shard_map/all_gather | solution.py:179
  99.2 90.8 %all-gather.19.cloned.1.call-start = ((), (), s32[]{:S(2)}) async-start(), calls=%async_computation.10 | async-start | bytes 3145728 | tf_op jit(solution)/shard_map/all_gather | solution.py:153
  99.8 1.3 copy-start.19
  99.8 5.6 copy-start.20
  99.8 10.0 copy-start.18
  99.8 14.8 %copy-start.10 = (bf16[1,128,1024]{2,1,0:T(8,128)(2,1)S(1)}, bf16[1,128,1024]{2,1,0:T(8,128)(2,1)}, u32[]{:S(2)}) copy-start(bf16[1,128,1024]{2,1,0:T(8,128)(2,1)} %param.15) | copy-start | bytes 786436
  99.9 195.6 %all-gather.21.cloned.1.call-start = ((), (), s32[]{:S(2)}) async-start(), calls=%async_computation.11 | async-start | bytes 12582912 | tf_op jit(solution)/shard_map/all_gather | solution.py:155
  100.4 300.4 %all-gather.23.cloned.1.call-start = ((), (), s32[]{:S(2)}) async-start(), calls=%async_computation.12 | async-start | bytes 12582912 | tf_op jit(solution)/shard_map/all_gather | solution.py:157
  101.0 411.3 %all-gather.27.cloned.1.call-start = ((), (), s32[]{:S(2)}) async-start(), calls=%async_computation.16 | async-start | bytes 3145728 | tf_op jit(solution)/shard_map/all_gather | solution.py:247
  114.8 286.1 %copy-start.11 = (bf16[128,1024]{1,0:T(8,128)(2,1)}, bf16[128,1024]{1,0:T(8,128)(2,1)S(1)}, u32[]{:S(2)}) copy-start(bf16[128,1024]{1,0:T(8,128)(2,1)S(1)} %get-tuple-element.37) | copy-start | bytes 786436
  115.0 43.6 %copy-start.14 = (bf16[128,1024]{0,1:T(8,128)(2,1)}, bf16[128,1024]{0,1:T(8,128)(2,1)S(1)}, u32[]{:S(2)}) copy-start(bf16[128,1024]{0,1:T(8,128)(2,1)S(1)} %copy.52) | copy-start | bytes 786436
  128.1 31.6 %copy-start.5 = (bf16[512,1024]{0,1:T(8,128)(2,1)}, bf16[512,1024]{0,1:T(8,128)(2,1)S(1)}, u32[]{:S(2)}) copy-start(bf16[512,1024]{0,1:T(8,128)(2,1)S(1)} %copy.51) | copy-start | bytes 3145732
  158.5 2.0 copy-start
  409.4 109.3 %reduce-scatter.5.cloned.1.call-start = ((), (), s32[]{:S(2)}) async-start(), calls=%async_computation.14 | async-start | bytes 2621440 | tf_op jit(solution)/shard_map/reduce_scatter | solution.py:215
  409.6 6.9 copy-start.1
  416.5 2.5 copy-start.3
  424.5 4.1 copy-start.15
  424.5 110.3 %reduce-scatter.3.cloned.1.call-start = ((), (), s32[]{:S(2)}) async-start(), calls=%async_computation.13 | async-start | bytes 2621440 | tf_op jit(solution)/shard_map/reduce_scatter | solution.py:214
  428.6 19.6 %copy-start.12 = (bf16[128,1024]{1,0:T(8,128)(2,1)S(1)}, bf16[128,1024]{1,0:T(8,128)(2,1)}, u32[]{:S(2)}) copy-start(bf16[128,1024]{1,0:T(8,128)(2,1)} %copy-done.11) | copy-start | bytes 786436
  460.6 14.3 %all-to-all-start.2 = ((bf16[128,2,512]{2,0,1:T(8,128)(2,1)}), bf16[128,2,512]{2,0,1:T(8,128)(2,1)S(1)}, u32[]{:S(2)}, u32[]{:S(2)}) async-start(bf16[128,2,512]{2,0,1:T(8,128)(2,1)} %copy.57), calls=%async_computation.4 | async-start | bytes 524288 | tf_op jit(solution)/shard_map/all_to_all | solution.py:243
  475.0 0.7 copy-start.13
  475.7 24.4 %all-to-all-start.4 = ((bf16[128,2,2048]{2,0,1:T(8,128)(2,1)}), bf16[128,2,2048]{2,0,1:T(8,128)(2,1)S(1)}, u32[]{:S(2)}, u32[]{:S(2)}) async-start(bf16[128,2,2048]{2,0,1:T(8,128)(2,1)} %bitcast.114), calls=%async_computation.6 | async-start | bytes 2097152 | tf_op jit(solution)/shard_map/all_to_all | solution.py:242
  479.3 18.0 %copy-start.7 = (bf16[256,1024]{1,0:T(8,128)(2,1)S(1)}, bf16[256,1024]{1,0:T(8,128)(2,1)}, u32[]{:S(2)}) copy-start(bf16[256,1024]{1,0:T(8,128)(2,1)} %all_gather.69) | copy-start | bytes 1572868
  500.0 8.8 all-to-all-start.3
  508.9 73.9 %all-to-all-start.1 = ((bf16[128,2,512]{2,0,1:T(8,128)(2,1)}), bf16[128,2,512]{2,0,1:T(8,128)(2,1)S(1)}, u32[]{:S(2)}, u32[]{:S(2)}) async-start(bf16[128,2,512]{2,0,1:T(8,128)(2,1)} %fusion.42), calls=%async_computation.3 | async-start | bytes 524288 | tf_op jit(solution)/shard_map/all_to_all | solution.py:240
  512.3 70.4 %all-gather.25.cloned.1.call-start = ((), (), s32[]{:S(2)}) async-start(), calls=%async_computation.15 | async-start | bytes 2359296 | tf_op jit(solution)/shard_map/all_gather | solution.py:246
  512.4 23.6 %copy-start.16 = (bf16[16,64,128]{2,1,0:T(8,128)(2,1)S(1)}, bf16[16,64,128]{2,1,0:T(8,128)(2,1)}, u32[]{:S(2)}) copy-start(bf16[16,64,128]{2,1,0:T(8,128)(2,1)} %get-tuple-element.72) | copy-start | bytes 786436
  536.9 5.3 copy-start.8
  536.9 5.3 copy-start.9
  536.9 683.3 %all-reduce.11.cloned.1.call-start = ((), (), s32[]{:S(2)}) async-start(), calls=%async_computation.17 | async-start | bytes 75497472 | tf_op jit(solution)/shard_map/psum | solution.py:279
  587.9 84.9 %copy-start.17 = (bf16[1,1024]{1,0:T(2,128)(2,1)S(1)}, bf16[1,1024]{1,0:T(2,128)(2,1)}, u32[]{:S(2)}) copy-start(bf16[1,1024]{1,0:T(2,128)(2,1)} %param.14) | copy-start | bytes 6148
  607.3 65.5 %all-to-all-start = ((f32[2,1,512]{2,1,0:T(1,128)}), f32[2,1,512]{2,1,0:T(1,128)S(1)}, u32[]{:S(2)}, u32[]{:S(2)}) async-start(f32[2,1,512]{2,1,0:T(1,128)} %copy.55), calls=%async_computation.2 | async-start | bytes 8192 | tf_op jit(solution)/shard_map/all_to_all | solution.py:277
  1231.0 6.9 copy-start.6
  1231.0 8.6 copy-start.4
  1237.9 6.0 slice-start
  1239.6 5.8 slice-start.1
Sparse Core Ops, SparseCore 0:
  9.5 84.1 all-gather.12
  98.5 28.0 all-gather.14
  128.8 27.3 all-gather.16
  157.6 32.4 all-gather.18
  191.4 103.9 all-gather.20
  296.9 103.9 all-gather.22
  409.5 33.0 all-gather.26
  445.5 43.6 reduce-scatter.4
  492.0 42.8 reduce-scatter.2
  537.0 27.5 all-gather.24
  588.0 632.1 all-reduce.10
where the time goes:
time: 1260 us
  waiting for transfers between devices  885 us (70%)
  blocking collectives  157 us (12%)
  matrix products  124 us (10%)
  local copies, waits for them, and re-layouts  43 us (3%)
  starting transfers between devices  18 us (1%)
  between operations  17.2 us (1%)
    psum x1, waiting for transfers between devices, local(): lax.psum((ada_shard, adab_shard, qkv_shard, qv_shard, proj_shard, projb_s...  547 us
    all_gather x1, waiting for transfers between devices, local(): lax.all_gather(fc1_weight, 'fsdp', axis=0, tiled=True)  101 us
    all_gather x1, waiting for transfers between devices, local(): lax.all_gather(fc2_weight, 'fsdp', axis=0, tiled=True)  98.7 us
    psum x1, blocking collectives, local(): lax.psum((ada_shard, adab_shard, qkv_shard, qv_shard, proj_shard, projb_s...  62.2 us
    all_gather x1, waiting for transfers between devices, local(): lax.all_gather(qkv_weight, 'fsdp', axis=0, tiled=True)  53.5 us
    unnamed x65, local copies, waits for them, and re-layouts  32.3 us
    all_gather x1, blocking collectives, local(): lax.all_gather(mods_grad[None, :], ('fsdp', 'seq'), axis=0, tiled=True)  31.1 us
    all_gather x1, waiting for transfers between devices, local(): lax.all_gather(key_rows, 'seq', axis=0, tiled=True)  28 us
  transfers between devices with their start and end apart: 16, of which 9 were waited for; matrix products, arithmetic and copies ran while one was open for 10% of the time, Pallas kernels for 0%

commit v1 on v0

--- a/solution.py
+++ b/solution.py
@@ -276,21 +276,20 @@
     )
     cond_sum = lax.all_to_all(cond_part, "fsdp", split_axis=0, concat_axis=1, tiled=True)
     cond_grad = cond_sum * silu_slope(cond_f)
-    sums = lax.psum(
-        (
-            ada_shard,
-            adab_shard,
-            qkv_shard,
-            qv_shard,
-            proj_shard,
-            projb_shard,
-            fc1_shard,
-            fc1b_shard,
-            fc2_shard,
-            fc2b_shard,
-        ),
-        ("rep", "seq"),
-    )
+    sums = (
+        ada_shard,
+        adab_shard,
+        qkv_shard,
+        qv_shard,
+        proj_shard,
+        projb_shard,
+        fc1_shard,
+        fc1b_shard,
+        fc2_shard,
+        fc2b_shard,
+    )
+    for over in ("seq", "rep"):
+        sums = lax.psum(sums, over)
     return (
         output[None],
         tokens_grad[None],

time: 1260 us -> 2500 us (1.98)
  waiting for transfers between devices: 885 us -> 2150 us
  blocking collectives: 157 us -> 124 us
    psum x1 -> x2, waiting for transfers between devices: 547 us -> 1820 us  [local(): sums = lax.psum(sums, over)]
    psum x1 -> x2, blocking collectives: 62.2 us -> 28.7 us  [local(): sums = lax.psum(sums, over)]
  transfers between devices with their start and end apart: 16 -> 17, of which waited for: 9 -> 10; matrix products, arithmetic and copies ran while one was open for 10% -> 5% of each run, Pallas kernels for 0% -> 0%
where the time goes in v1:
time: 2500 us; the launch traced here: 2490 us
  waiting for transfers between devices  2150 us (86%)
  blocking collectives  124 us (5%)
  matrix products  123 us (5%)
  local copies, waits for them, and re-layouts  43 us (2%)
    psum x2, waiting for transfers between devices, local(): sums = lax.psum(sums, over)  1820 us
    all_gather x1, waiting for transfers between devices, local(): lax.all_gather(fc1_weight, 'fsdp', axis=0, tiled=True)  101 us
    all_gather x1, waiting for transfers between devices, local(): lax.all_gather(fc2_weight, 'fsdp', axis=0, tiled=True)  98.7 us
    all_gather x1, waiting for transfers between devices, local(): lax.all_gather(qkv_weight, 'fsdp', axis=0, tiled=True)  53.5 us
  transfers between devices with their start and end apart: 17, of which 10 were waited for; matrix products, arithmetic and copies ran while one was open for 5% of the time, Pallas kernels for 0%

profile of v1, /device:TPU:0, one launch (start us, length us, event | category | flops | bytes accessed | tf_op | source)
XLA Modules:
  0.0 2491.4 jit_solution(13890675977704296122)
XLA Ops:
  8.0 1.2 dynamic-slice.1
  9.2 5.5 all_gather.58
  15.4 4.4 all-gather.1
  19.8 4.6 all_gather.56
  24.4 4.3 fusion.54
  28.7 10.4 all-reduce
  40.2 53.5 %all-gather.13.cloned.1.call-done = bf16[1024,3072]{1,0:T(8,128)(2,1)} async-done(((bf16[512,3072]{1,0:T(8,128)(2,1)}), bf16[1024,3072]{1,0:T(8,128)(2,1)}) %all-gather.13.cloned.1.call-update) | async-done | bytes 6291472 | tf_op jit(solution)/shard_map/all_gather | solution.py:151
  93.7 3.9 fusion.44
  101.1 4.4 all-gather.2
  105.5 4.4 all-gather.3
  109.9 4.8 all_gather.64
  115.0 11.7 all-gather.15.cloned.1.call-done
  126.6 1.5 copy.51
  128.1 28.0 %all-gather.17.cloned.1.call-done = bf16[512,1024]{1,0:T(8,128)(2,1)} async-done(((bf16[128,1024]{1,0:T(8,128)(2,1)}), bf16[512,1024]{1,0:T(8,128)(2,1)}) %all-gather.17.cloned.1.call-update) | async-done | bytes 1048592 | tf_op jit(solution)/shard_map/all_gather | solution.py:179
  156.2 1.5 copy.53
  158.5 1.2 fusion.3
  160.5 2.2 fusion.31
  162.7 27.4 %all-gather.19.cloned.1.call-done = bf16[1024,1024]{1,0:T(8,128)(2,1)} async-done(((bf16[512,1024]{1,0:T(8,128)(2,1)}), bf16[1024,1024]{1,0:T(8,128)(2,1)}) %all-gather.19.cloned.1.call-update) | async-done | bytes 2097168 | tf_op jit(solution)/shard_map/all_gather | solution.py:153
  190.1 3.0 fusion.68
  194.1 101.3 %all-gather.21.cloned.1.call-done = bf16[1024,4096]{1,0:T(8,128)(2,1)} async-done(((bf16[512,4096]{1,0:T(8,128)(2,1)}), bf16[1024,4096]{1,0:T(8,128)(2,1)}) %all-gather.21.cloned.1.call-update) | async-done | bytes 8388624 | tf_op jit(solution)/shard_map/all_gather | solution.py:155
  295.5 6.7 multiply_convert_fusion.1
  302.1 98.7 %all-gather.23.cloned.1.call-done = bf16[4096,1024]{1,0:T(8,128)(2,1)} async-done(((bf16[2048,1024]{1,0:T(8,128)(2,1)}), bf16[4096,1024]{1,0:T(8,128)(2,1)}) %all-gather.23.cloned.1.call-update) | async-done | bytes 8388624 | tf_op jit(solution)/shard_map/all_gather | solution.py:157
  400.9 8.5 convert_reduce_fusion
  409.6 6.9 multiply_reduce_fusion.2
  416.5 2.5 fusion.36
  420.0 4.5 fusion.13
  424.6 4.0 fusion.73
  428.6 18.3 fusion.8
  446.9 1.3 reshape.183
  448.2 8.5 all_gather.71
  456.7 2.1 fusion.42
  458.8 1.8 copy.57
  460.6 3.4 all-to-all-start.2
  464.1 1.7 copy.88
  465.8 1.0 copy.87
  466.8 8.2 all_gather.69
  475.7 3.6 all-to-all-start.4
  479.3 18.0 convert_reduce_fusion.4
  497.2 2.8 fusion.75
  500.0 3.7 all-to-all-start.3
  503.7 4.7 fusion.77
  508.8 3.4 all-to-all-start.1
  512.4 6.3 fusion.76
  518.7 1.2 convert_reduce_fusion.3
  519.9 15.0 reduce-scatter.3.cloned.1.call-done
  534.9 1.1 convert_element_type.161
  537.0 5.2 multiply_reduce_fusion.4
  542.3 1.1 multiply_reduce_fusion.3
  543.4 31.1 %all-gather = f32[49152]{0:T(1024)S(1)} all-gather(f32[6144]{0:T(1024)S(1)} %constant_dynamic-update-slice_fusion), channel_id=2, replica_groups=mesh['rep'=4,'fsdp'=2,'seq'=4] {'fsdp','seq'}, dimensions={0}, use_global_device_ids=true | all-gather | bytes 221184 | tf_op jit(solution)/shard_map/all_gather | solution.py:262
  574.7 8.1 fusion.50
  582.7 5.1 fusion.74
  587.9 1239.0 %all-reduce.14.cloned.1.call-done = (f32[512,6144]{1,0:T(8,128)}, f32[512,3072]{1,0:T(8,128)}, f32[512,1024]{1,0:T(8,128)}, f32[512,4096]{1,0:T(8,128)}, f32[2048,1024]{1,0:T(8,128)}) async-done(((f32[512,6144]{1,0:T(8,128)}, f32[512,3072]{1,0:T(8,128)}, f32[512,1024]{1,0:T(8,128)}, f32[512,4096]{1,0:T(8,128)}, f32[2048,1024]{1,0:T(8,128)}), (f32[512,6144]{1,0:T(8,128)}, f32[512,3072]{1,0:T(8,128)}, ...) | async-done | bytes 37748752 | tf_op jit(solution)/shard_map/psum | solution.py:292
  1829.6 8.8 all-reduce.10
  1838.7 7.0 convolution_bitcast_fusion
  1846.3 3.2 all-to-all-start
  1849.6 15.9 all-reduce.6
  1865.5 12.8 all-reduce.8
  1878.9 576.8 %all-reduce.16.cloned.1.call-done = (f32[512,6144]{1,0:T(8,128)}, f32[512,3072]{1,0:T(8,128)}, f32[512,1024]{1,0:T(8,128)}, f32[512,4096]{1,0:T(8,128)}, f32[2048,1024]{1,0:T(8,128)}) async-done(((f32[512,6144]{1,0:T(8,128)}, f32[512,3072]{1,0:T(8,128)}, f32[512,1024]{1,0:T(8,128)}, f32[512,4096]{1,0:T(8,128)}, f32[2048,1024]{1,0:T(8,128)}), (f32[512,6144]{1,0:T(8,128)}, f32[512,3072]{1,0:T(8,128)}, ...) | async-done | bytes 37748752 | tf_op jit(solution)/shard_map/psum | solution.py:292
  2455.7 10.8 copy.104
  2466.6 6.9 copy.105
  2473.4 1.3 copy.106
  2475.2 4.3 copy.107
  2479.4 1.5 slice-done.1
  2480.9 3.4 copy.108
  (129 shorter events, 14.7 us)
Async XLA Ops:
  7.2 31.9 %copy-start.2 = (bf16[1,128,1024]{2,1,0:T(8,128)(2,1)S(1)}, bf16[1,128,1024]{2,1,0:T(8,128)(2,1)}, u32[]{:S(2)}) copy-start(bf16[1,128,1024]{2,1,0:T(8,128)(2,1)} %param.13) | copy-start | bytes 786436
  7.2 86.5 %all-gather.13.cloned.1.call-start = ((), (), s32[]{:S(2)}) async-start(), calls=%async_computation.7 | async-start | bytes 9437184 | tf_op jit(solution)/shard_map/all_gather | solution.py:151
  7.9 118.7 %all-gather.15.cloned.1.call-start = ((), (), s32[]{:S(2)}) async-start(), calls=%async_computation.8 | async-start | bytes 1310720 | tf_op jit(solution)/shard_map/all_gather | solution.py:180
  98.4 57.7 %all-gather.17.cloned.1.call-start = ((), (), s32[]{:S(2)}) async-start(), calls=%async_computation.9 | async-start | bytes 1310720 | tf_op jit(solution)/shard_map/all_gather | solution.py:179
  99.2 90.8 %all-gather.19.cloned.1.call-start = ((), (), s32[]{:S(2)}) async-start(), calls=%async_computation.10 | async-start | bytes 3145728 | tf_op jit(solution)/shard_map/all_gather | solution.py:153
  99.8 1.3 copy-start.19
  99.8 5.6 copy-start.20
  99.8 10.0 copy-start.18
  99.8 14.8 copy-start.10
  99.9 195.6 %all-gather.21.cloned.1.call-start = ((), (), s32[]{:S(2)}) async-start(), calls=%async_computation.11 | async-start | bytes 12582912 | tf_op jit(solution)/shard_map/all_gather | solution.py:155
  100.4 300.4 %all-gather.23.cloned.1.call-start = ((), (), s32[]{:S(2)}) async-start(), calls=%async_computation.12 | async-start | bytes 12582912 | tf_op jit(solution)/shard_map/all_gather | solution.py:157
  101.0 411.3 %all-gather.27.cloned.1.call-start = ((), (), s32[]{:S(2)}) async-start(), calls=%async_computation.16 | async-start | bytes 3145728 | tf_op jit(solution)/shard_map/all_gather | solution.py:247
  114.8 286.1 %copy-start.11 = (bf16[128,1024]{1,0:T(8,128)(2,1)}, bf16[128,1024]{1,0:T(8,128)(2,1)S(1)}, u32[]{:S(2)}) copy-start(bf16[128,1024]{1,0:T(8,128)(2,1)S(1)} %get-tuple-element.47) | copy-start | bytes 786436
  115.0 43.6 %copy-start.14 = (bf16[128,1024]{0,1:T(8,128)(2,1)}, bf16[128,1024]{0,1:T(8,128)(2,1)S(1)}, u32[]{:S(2)}) copy-start(bf16[128,1024]{0,1:T(8,128)(2,1)S(1)} %copy.52) | copy-start | bytes 786436
  128.1 31.6 %copy-start.5 = (bf16[512,1024]{0,1:T(8,128)(2,1)}, bf16[512,1024]{0,1:T(8,128)(2,1)S(1)}, u32[]{:S(2)}) copy-start(bf16[512,1024]{0,1:T(8,128)(2,1)S(1)} %copy.51) | copy-start | bytes 3145732
  158.5 2.0 copy-start
  409.4 109.3 %reduce-scatter.5.cloned.1.call-start = ((), (), s32[]{:S(2)}) async-start(), calls=%async_computation.14 | async-start | bytes 2621440 | tf_op jit(solution)/shard_map/reduce_scatter | solution.py:215
  409.6 6.9 copy-start.1
  416.5 2.5 copy-start.3
  424.5 4.1 copy-start.15
  424.5 110.4 %reduce-scatter.3.cloned.1.call-start = ((), (), s32[]{:S(2)}) async-start(), calls=%async_computation.13 | async-start | bytes 2621440 | tf_op jit(solution)/shard_map/reduce_scatter | solution.py:214
  428.6 19.6 copy-start.12
  460.6 14.3 all-to-all-start.2
  474.9 0.7 copy-start.13
  475.7 24.3 all-to-all-start.4
  479.3 18.0 copy-start.7
  500.0 8.8 all-to-all-start.3
  508.8 73.9 %all-to-all-start.1 = ((bf16[128,2,512]{2,0,1:T(8,128)(2,1)}), bf16[128,2,512]{2,0,1:T(8,128)(2,1)S(1)}, u32[]{:S(2)}, u32[]{:S(2)}) async-start(bf16[128,2,512]{2,0,1:T(8,128)(2,1)} %fusion.42), calls=%async_computation.3 | async-start | bytes 524288 | tf_op jit(solution)/shard_map/all_to_all | solution.py:240
  512.3 70.5 %all-gather.25.cloned.1.call-start = ((), (), s32[]{:S(2)}) async-start(), calls=%async_computation.15 | async-start | bytes 2359296 | tf_op jit(solution)/shard_map/all_gather | solution.py:246
  512.3 23.6 copy-start.16
  536.9 5.3 copy-start.8
  537.0 5.3 copy-start.9
  537.0 1290.0 %all-reduce.14.cloned.1.call-start = ((), (), s32[]{:S(2)}) async-start(), calls=%async_computation.17 | async-start | bytes 75497472 | tf_op jit(solution)/shard_map/psum | solution.py:292
  587.9 1867.8 %all-reduce.16.cloned.1.call-start = ((), (), s32[]{:S(2)}) async-start(), calls=%async_computation.18 | async-start | bytes 75497472 | tf_op jit(solution)/shard_map/psum | solution.py:292
  1826.9 51.4 %copy-start.17 = (bf16[1,1024]{1,0:T(2,128)(2,1)S(1)}, bf16[1,1024]{1,0:T(2,128)(2,1)}, u32[]{:S(2)}) copy-start(bf16[1,1024]{1,0:T(2,128)(2,1)} %param.14) | copy-start | bytes 6148
  1846.3 32.0 %all-to-all-start = ((f32[2,1,512]{2,1,0:T(1,128)}), f32[2,1,512]{2,1,0:T(1,128)S(1)}, u32[]{:S(2)}, u32[]{:S(2)}) async-start(f32[2,1,512]{2,1,0:T(1,128)} %copy.55), calls=%async_computation.2 | async-start | bytes 8192 | tf_op jit(solution)/shard_map/all_to_all | solution.py:277
  2466.6 6.9 copy-start.6
  2466.6 8.6 copy-start.4
  2473.4 6.0 slice-start
  2475.2 5.8 slice-start.1
Sparse Core Ops, SparseCore 0:
  9.5 84.1 all-gather.12
  98.5 28.0 all-gather.14
  128.8 27.3 all-gather.16
  157.6 32.4 all-gather.18
  191.4 103.9 all-gather.20
  296.9 103.9 all-gather.22
  409.5 33.0 all-gather.26
  445.5 43.6 reduce-scatter.4
  492.0 42.8 reduce-scatter.2
  537.1 27.5 all-gather.24
  588.0 1238.8 all-reduce.13
  1829.8 625.8 all-reduce.15
